TPU v7x, 512 devices: a whole 4x8x8 slice. The times are simulated.
512 devices in a mesh: expert: 32 (over y, x), tensor: 16 (over z, core).
Axes of the slice: x: 4, y: 8, z: 8, core: 2. Of those that a mesh axis runs over, the one named last changes fastest.
Arguments:
- residual: bfloat16 [2048, 7168], P('expert', 'tensor'), may hold values from -40 to 40
- attn_parts: bfloat16 [16, 2048, 7168], P('tensor', 'expert'), may hold values from -2 to 2
- norm_gain: bfloat16 [7168], P('tensor'), may hold values from 0.099609375 to 1.8984375
- routes: int32 [2048, 8], P('expert'), may hold values from 0 to 31, all different within a row; in each aligned block of 64 rows (0 to 63, 64 to 127, ...) at most 24 rows name the same one
- route_weights: float32 [2048, 8], P('expert'), may hold values from 0.05 to 0.6
- w_gate: bfloat16 [32, 7168, 2048], P('expert', None, 'tensor'), may hold values from -0.06023809 to 0.06023809
- w_gate_q: bfloat16 [32, 7168, 2048], P('expert', None, 'tensor'), may hold values from -0.09567226 to 0.09567226
Outputs:
- token_error: float32 [2048], P('expert')
- expert_error: float32 [32], P('expert')
- hess_diag: float32 [32, 7168], P('expert', 'tensor')
Inputs may be any that keep to these rules, and one draw needn't show every extreme that they name: `routes`: no expert is named by more than 24 of the rows of one device, and in every draw some expert is named by exactly 24 of them; the 8 experts of a token are distinct; every expert is named by some token.
All inputs are finite; a program needn't handle non-finite values.
Results may differ from a plain program's by a relative error of at most 0.0023.
Values may be sent and summed in bfloat16 or wider, within the bound.
A program may use at most 64 MiB of HBM per device.

v0:
```python
import jax
import jax.numpy as jnp
from jax import lax
from jax.sharding import PartitionSpec as P

D = 7168
FF = 2048
CAP = 24
epsilon = 1e-06


def per_device(residual, attn_parts, norm_gain, routes, route_weights, w_gate, w_gate_q):
    n_expert = lax.axis_size("expert")
    tok_count = residual.shape[0]
    local_cols = residual.shape[1]
    top_count = routes.shape[1]
    gain_local = norm_gain.astype(jnp.float32)[None, :]
    gain_full = lax.all_gather(norm_gain, "tensor", tiled=True).astype(jnp.float32)[None, :]
    summed = lax.psum_scatter(
        attn_parts[0].astype(jnp.float32).astype(jnp.bfloat16),
        "tensor",
        scatter_dimension=1,
        tiled=True,
    ).astype(jnp.float32)
    hidden = (residual.astype(jnp.float32) + summed).astype(jnp.bfloat16)
    expert_ids = jnp.arange(n_expert, dtype=jnp.int32)
    flat_routes = routes.reshape(-1)
    one_hot = (flat_routes[:, None] == expert_ids[None, :]).astype(jnp.int32)
    earlier = jnp.cumsum(one_hot, axis=0) - one_hot
    slot_index = jnp.sum(earlier * one_hot, axis=1)
    target = flat_routes * CAP + slot_index
    load_counts = jnp.sum(one_hot, axis=0)
    slot_ids = jnp.arange(n_expert * CAP, dtype=jnp.int32)
    placing = (slot_ids[:, None] == target[None, :]).reshape(n_expert * CAP, tok_count, top_count)
    dispatch = jnp.sum(placing.astype(jnp.int32), axis=2).astype(jnp.bfloat16)
    outgoing = jnp.dot(dispatch, hidden, preferred_element_type=jnp.float32).astype(jnp.bfloat16)
    outgoing = outgoing.reshape(n_expert, CAP, local_cols)
    count_rows = jnp.broadcast_to(
        load_counts.astype(jnp.bfloat16)[:, None, None], (n_expert, 1, local_cols)
    )
    outgoing = jnp.concatenate([outgoing, count_rows], axis=1)
    arrived = lax.all_to_all(outgoing, "expert", split_axis=0, concat_axis=0, tiled=True)
    arrived_counts = arrived[:, CAP, 0].astype(jnp.float32)
    own_block = arrived[:, :CAP, :].reshape(n_expert * CAP, local_cols)
    column_block = lax.all_gather(own_block, "tensor", axis=1, tiled=True)
    wide = column_block.astype(jnp.float32)
    scaling = lax.rsqrt(jnp.sum(wide * wide, axis=1, keepdims=True) / D + epsilon)
    normed = (wide * scaling * gain_full).astype(jnp.bfloat16)
    normed_local = (own_block.astype(jnp.float32) * scaling * gain_local).astype(jnp.bfloat16)
    full_acc = jnp.dot(normed, w_gate[0], preferred_element_type=jnp.float32)
    quant_acc = jnp.dot(normed, w_gate_q[0], preferred_element_type=jnp.float32)
    block_squares = jnp.einsum(
        "rc,rc->c", normed_local, normed_local, preferred_element_type=jnp.float32
    )
    total_load = jnp.sum(arrived_counts)
    hess_local = 2.0 * block_squares / total_load
    difference = full_acc - quant_acc
    err_part = (jnp.sum(difference * difference, axis=1) / FF).reshape(n_expert, 1, CAP)
    pow_part = (jnp.sum(full_acc * full_acc, axis=1) / FF).reshape(n_expert, 1, CAP)
    slots = lax.psum(jnp.concatenate([err_part, pow_part], axis=1), "tensor")
    expert_total = jnp.sum(slots[:, 0]) / (jnp.sum(slots[:, 1]) + epsilon)
    back = lax.all_to_all(slots, "expert", split_axis=0, concat_axis=0, tiled=True)
    token_err = jnp.take(back[:, 0].reshape(-1), target).reshape(tok_count, top_count)
    token_pow = jnp.take(back[:, 1].reshape(-1), target).reshape(tok_count, top_count)
    ratios = token_err / (token_pow + epsilon)
    token_error = jnp.sum(route_weights * ratios, axis=1)
    return (token_error, expert_total.reshape(1), hess_local.reshape(1, local_cols))


def solution(mesh):
    placed = (
        P("expert", "tensor"),
        P("tensor", "expert", None),
        P("tensor"),
        P("expert", None),
        P("expert", None),
        P("expert", None, "tensor"),
        P("expert", None, "tensor"),
    )
    return jax.shard_map(
        per_device,
        mesh=mesh,
        in_specs=placed,
        out_specs=(P("expert"), P("expert"), P("expert", "tensor")),
        check_vma=False,
    )
```

profile of v0, /device:TPU:2, one launch (start us, length us, event | category | flops | bytes accessed | tf_op | source)
XLA Modules:
  0.0 279.3 jit_solution(10890716168880705273)
XLA Ops:
  7.2 0.0 copy-start
  7.2 0.0 reduce-scatter.4.cloned.1.call-start
  7.2 0.0 copy-start.5
  7.2 2.8 copy.51
  10.0 0.0 copy-start.4
  10.0 0.0 reduce-scatter.4.cloned.1.call-update
  10.0 0.0 all-gather.2.cloned.1.call-start
  10.1 0.0 copy-done.5
  10.1 0.1 copy.36
  10.2 0.1 eq.40
  10.3 0.1 eq.44
  10.4 1.2 reduce-window.6
  11.5 0.2 slice_reduce_fusion
  11.8 0.2 fusion.28
  11.9 0.1 reduce_sum.93
  12.0 0.1 copy.39
  12.1 0.1 copy.40
  12.2 0.5 convert_reduce_fusion
  12.7 65.0 %reduce-scatter.4.cloned.1.call-done = bf16[448,64]{1,0:T(8,128)(2,1)} async-done(((bf16[7168,64]{1,0:T(8,128)(2,1)}), bf16[448,64]{1,0:T(8,128)(2,1)}) %reduce-scatter.4.cloned.1.call-update) | async-done | bytes 57360
  77.8 1.0 copy.52
  78.8 0.0 copy-done.4
  78.8 0.4 convolution_convert_fusion
  79.2 0.3 copy.41
  79.5 0.1 broadcast_in_dim.6
  79.6 0.2 pad_maximum_fusion
  79.8 34.8 %all_to_all.10 = bf16[32,25,448]{2,1,0:T(8,128)(2,1)S(1)} all-to-all(bf16[32,25,448]{2,1,0:T(8,128)(2,1)S(1)} %pad_maximum_fusion), channel_id=1, replica_groups=mesh['expert'=32,'tensor'=16] {'expert'}, dimensions={0} | all-to-all | bytes 1433600 | tf_op jit(solution)/shard_map/all_to_all | solution.py:42
  114.5 0.0 copy-start.3
  114.5 1.0 copy-done.3
  115.5 0.1 slice.37
  115.6 0.0 copy-start.2
  115.6 1.2 copy.42
  116.8 0.0 all-gather.2.cloned.1.call-update
  116.8 0.0 copy-done.7
  116.8 1.3 dynamic-slice
  118.8 0.3 dynamic-update-slice
  119.0 51.5 %all-reduce = bf16[7168]{0:T(1024)(128)(2,1)S(1)} all-reduce(bf16[7168]{0:T(1024)(128)(2,1)S(1)} %dynamic-update-slice), channel_id=1, replica_groups=mesh['expert'=32,'tensor'=16] {'tensor'}, use_global_device_ids=true, to_apply=%add | all-reduce | flops 7168 | bytes 28672
  170.5 0.0 copy-done.6
  170.5 0.1 copy.44
  170.6 1.5 fusion.30
  172.1 0.0 copy-done.2
  172.1 13.0 %all-gather.2.cloned.1.call-done = bf16[768,7168]{0,1:T(8,128)(2,1)} async-done(((bf16[768,448]{0,1:T(8,128)(2,1)}), bf16[768,7168]{0,1:T(8,128)(2,1)}) %all-gather.2.cloned.1.call-update) | async-done | bytes 11010064 | tf_op jit(solution)/shard_map/all_gather | solution.py:45
  185.1 6.5 %fusion = f32[768]{0:T(1024)S(1)} fusion(bf16[768,7168]{0,1:T(8,128)(2,1)} %all-gather.2.cloned.1.call-done), kind=kLoop, calls=%fused_computation.4 | loop fusion | flops 16514304 | bytes 11013120 | tf_op jit(solution)/shard_map/reduce_sum | solution.py:47
  191.6 1.5 fusion.9
  193.1 0.0 copy-done
  193.1 0.0 copy-done.1
  193.1 0.0 copy-start.8
  193.1 3.3 %multiply_reduce_fusion = (f32[768]{0:T(1024)S(1)}, f32[768,128]{0,1:T(8,128)S(1)}) fusion(bf16[1,7168,128]{2,1,0:T(8,128)(2,1)S(1)} %copy-done, bf16[768,7168]{0,1:T(8,128)(2,1)S(1)} %copy-done.1, f32[7168]{0:T(1024)S(1)} %convert_element_type.66, f32[768]{0:T(1024)S(1)} %add_rsqrt_fusion), kind=kOutput, calls=%fused_computation.22 | convolution fusion | flops 1431502080 | bytes 13273088 | tf_op jit(solution)/shard_map/dot_general | solution.py:50
  196.5 0.0 copy-done.8
  196.5 3.4 %fusion.20 = f32[768]{0:T(1024)S(1)} fusion(f32[768,128]{0,1:T(8,128)S(1)} %get-tuple-element.11, bf16[1,7168,128]{2,1,0:T(8,128)(2,1)S(1)} %copy-done.8, bf16[768,7168]{0,1:T(8,128)(2,1)S(1)} %copy-done.1, f32[7168]{0:T(1024)S(1)} %convert_element_type.66, f32[768]{0:T(1024)S(1)} %add_rsqrt_fusion), kind=kOutput, calls=%fused_computation.19 | convolution fusion | flops 1431600384 | bytes 13273088 | tf_op jit(solution)/shard_map/dot_general | solution.py:51
  199.8 0.1 div.34
  199.9 0.1 div.36
  200.0 46.7 %psum.7 = f32[32,2,24]{2,0,1:T(8,128)S(1)} all-reduce(f32[32,2,24]{2,0,1:T(8,128)S(1)} %pad_maximum_fusion.1), channel_id=1, replica_groups=mesh['expert'=32,'tensor'=16] {'tensor'}, use_global_device_ids=true, to_apply=%region_9.10 | all-reduce | flops 1536 | bytes 12288 | tf_op jit(solution)/shard_map/psum | solution.py:60
  246.7 0.6 copy.43
  247.4 9.8 %all-to-all-start.1 = ((f32[32,2,24]{2,1,0:T(2,128)}), f32[32,2,24]{2,1,0:T(2,128)S(1)}, u32[]{:S(2)}, u32[]{:S(2)}) async-start(f32[32,2,24]{2,1,0:T(2,128)} %copy.43), calls=%async_computation.1 | async-start | bytes 65536 | tf_op jit(solution)/shard_map/all_to_all | solution.py:62
  257.1 1.2 multiply_divide_fusion
  258.4 0.6 slice_reduce_fusion.1
  260.3 5.5 %all-to-all-done.1 = f32[32,2,24]{2,1,0:T(2,128)S(1)} async-done(((f32[32,2,24]{2,1,0:T(2,128)}), f32[32,2,24]{2,1,0:T(2,128)S(1)}, u32[]{:S(2)}, u32[]{:S(2)}) %all-to-all-start.1) | async-done | bytes 6176 | tf_op jit(solution)/shard_map/all_to_all | solution.py:62
  265.8 0.1 slice_reduce_fusion.4
  265.9 0.1 reshape_squeeze.6
  266.0 0.1 reshape_squeeze.7
  266.0 2.3 gather_fusion
  268.3 2.3 gather_fusion.1
  270.6 0.1 div.38
  270.7 0.6 multiply_reduce_fusion.1
  (18 shorter events, 0.1 us)
Async XLA Ops:
  7.2 186.0 %copy-start = (bf16[1,7168,128]{2,1,0:T(8,128)(2,1)S(1)}, bf16[1,7168,128]{2,1,0:T(8,128)(2,1)}, u32[]{:S(2)}) copy-start(bf16[1,7168,128]{2,1,0:T(8,128)(2,1)} %param.14) | copy-start | bytes 5505028
  7.2 70.6 %reduce-scatter.4.cloned.1.call-start = ((), (), s32[]{:S(2)}) async-start(), calls=%async_computation.4 | async-start | bytes 1949696
  7.2 2.8 %copy-start.5 = (s32[64,8]{0,1:T(8,128)S(1)}, s32[64,8]{0,1:T(8,128)}, u32[]{:S(2)}) copy-start(s32[64,8]{0,1:T(8,128)} %param.12) | copy-start | bytes 6148
  10.0 68.8 %copy-start.4 = (bf16[64,448]{1,0:T(8,128)(2,1)S(1)}, bf16[64,448]{1,0:T(8,128)(2,1)}, u32[]{:S(2)}) copy-start(bf16[64,448]{1,0:T(8,128)(2,1)} %param.9) | copy-start | bytes 172036
  10.0 175.1 %all-gather.2.cloned.1.call-start = ((), (), s32[]{:S(2)}) async-start(), calls=%async_computation.3 | async-start | bytes 11698176 | tf_op jit(solution)/shard_map/all_gather | solution.py:45
  114.5 1.0 copy-start.3
  115.5 1.3 copy-start.7
  115.5 55.0 %copy-start.6 = (f32[64,8]{0,1:T(8,128)S(1)}, f32[64,8]{0,1:T(8,128)}, u32[]{:S(2)}) copy-start(f32[64,8]{0,1:T(8,128)} %param.13) | copy-start | bytes 6148
  115.6 56.5 %copy-start.2 = (bf16[32,24,448]{2,1,0:T(8,128)(2,1)}, bf16[32,24,448]{2,1,0:T(8,128)(2,1)S(1)}, u32[]{:S(2)}) copy-start(bf16[32,24,448]{2,1,0:T(8,128)(2,1)S(1)} %slice.37) | copy-start | bytes 2064388
  185.1 8.0 %copy-start.1 = (bf16[768,7168]{0,1:T(8,128)(2,1)S(1)}, bf16[768,7168]{0,1:T(8,128)(2,1)}, u32[]{:S(2)}) copy-start(bf16[768,7168]{0,1:T(8,128)(2,1)} %all-gather.2.cloned.1.call-done) | copy-start | bytes 33030148
  193.1 3.3 %copy-start.8 = (bf16[1,7168,128]{2,1,0:T(8,128)(2,1)S(1)}, bf16[1,7168,128]{2,1,0:T(8,128)(2,1)}, u32[]{:S(2)}) copy-start(bf16[1,7168,128]{2,1,0:T(8,128)(2,1)} %param.15) | copy-start | bytes 5505028
  247.4 18.4 %all-to-all-start.1 = ((f32[32,2,24]{2,1,0:T(2,128)}), f32[32,2,24]{2,1,0:T(2,128)S(1)}, u32[]{:S(2)}, u32[]{:S(2)}) async-start(f32[32,2,24]{2,1,0:T(2,128)} %copy.43), calls=%async_computation.1 | async-start | bytes 65536 | tf_op jit(solution)/shard_map/all_to_all | solution.py:62
Sparse Core Ops, SparseCore 0:
  10.8 66.8 reduce-scatter.3
  116.9 68.1 all-gather.1
where the time goes:
time: 280 us; the launch traced here: 279 us
  blocking collectives  133 us (48%)
  waiting for transfers between devices  83.6 us (30%)
  between operations  17.4 us (6%)
  local copies, waits for them, and re-layouts  14.4 us (5%)
  other arithmetic  14.1 us (5%)
  starting transfers between devices  9.86 us (4%)
  matrix products  7.03 us (3%)
    unnamed x3, waiting for transfers between devices  65.1 us
    unnamed x1, blocking collectives  51.5 us
    psum x1, blocking collectives, per_device(): slots = lax.psum(jnp.concatenate([err_part, pow_part], axis=1), 'tensor')  46.7 us
    all_to_all x1, blocking collectives, per_device(): lax.all_to_all(outgoing, 'expert', split_axis=0, concat_axis=0, tiled=True)  34.8 us
    all_gather x1, waiting for transfers between devices, per_device(): column_block = lax.all_gather(own_block, 'tensor', axis=1, tiled=True)  13 us
    all_to_all x1, starting transfers between devices, per_device(): lax.all_to_all(slots, 'expert', split_axis=0, concat_axis=0, tiled=True)  9.77 us
    reduce_sum x1, other arithmetic, per_device(): jnp.sum(wide * wide, axis=1, keepdims=True) / D + epsilon  6.51 us
    unnamed x25, local copies, waits for them, and re-layouts  6.44 us
  transfers between devices with their start and end apart: 3, of which 3 were waited for; matrix products, arithmetic and copies ran while one was open for 3% of the time, Pallas kernels for 0%

commit v1 on v0

--- a/solution.py
+++ b/solution.py
@@ -42,7 +42,27 @@
     arrived = lax.all_to_all(outgoing, "expert", split_axis=0, concat_axis=0, tiled=True)
     arrived_counts = arrived[:, CAP, 0].astype(jnp.float32)
     own_block = arrived[:, :CAP, :].reshape(n_expert * CAP, local_cols)
-    column_block = lax.all_gather(own_block, "tensor", axis=1, tiled=True)
+    size, position, width = (lax.axis_size("tensor"), lax.axis_index("tensor"), own_block.shape[1])
+    ahead = [(i, (i + 1) % size) for i in range(size)]
+    downward = [(i, (i - 1) % size) for i in range(size)]
+    column_block = jnp.zeros(
+        (*own_block.shape[:1], size * width, *own_block.shape[1 + 1 :]), own_block.dtype
+    )
+    column_block = lax.dynamic_update_slice_in_dim(
+        column_block, own_block, position * width, axis=1
+    )
+    from_left = from_right = own_block
+    half = size // 2
+    for step in range(1, half + 1):
+        from_left = lax.ppermute(from_left, "tensor", ahead)
+        column_block = lax.dynamic_update_slice_in_dim(
+            column_block, from_left, (position - step) % size * width, axis=1
+        )
+        if step < size - half:
+            from_right = lax.ppermute(from_right, "tensor", downward)
+            column_block = lax.dynamic_update_slice_in_dim(
+                column_block, from_right, (position + step) % size * width, axis=1
+            )
     wide = column_block.astype(jnp.float32)
     scaling = lax.rsqrt(jnp.sum(wide * wide, axis=1, keepdims=True) / D + epsilon)
     normed = (wide * scaling * gain_full).astype(jnp.bfloat16)

time: 280 us -> 504 us (1.80)
  local copies, waits for them, and re-layouts: 14.4 us -> 175 us
  waiting for transfers between devices: 83.6 us -> 129 us
  starting transfers between devices: 9.86 us -> 23.2 us
    dynamic_update_slice x0 -> x16, local copies, waits for them, and re-layouts: none -> 132 us  [the longest x8 65.3 us: per_device(): lax.dynamic_update_slice_in_dim(column_block, from_left, (position - step...]
    ppermute x0 -> x15, waiting for transfers between devices: none -> 60.1 us  [the longest x8 60.1 us: per_device(): from_left = lax.ppermute(from_left, 'tensor', ahead)]
    ppermute x0 -> x15, local copies, waits for them, and re-layouts: none -> 19.5 us  [the longest x8 11 us: per_device(): from_left = lax.ppermute(from_left, 'tensor', ahead)]
    ppermute x0 -> x15, starting transfers between devices: none -> 17.6 us  [the longest x7 17.6 us: per_device(): from_right = lax.ppermute(from_right, 'tensor', downward)]
    all_gather x1 -> x0, waiting for transfers between devices: 13 us -> none  [per_device(): column_block = lax.all_gather(own_block, 'tensor', axis=1, tiled=True)]
    broadcast_in_dim x0 -> x1, local copies, waits for them, and re-layouts: none -> 5.53 us  [per_device(): jnp.zeros((*own_block.shape[:1], size * width, *own_block.shape[1 + 1:]),...]
    unnamed x25 -> x41, local copies, waits for them, and re-layouts: 6.44 us -> 10.4 us
    unnamed x3 -> x2, waiting for transfers between devices: 65.1 us -> 63.8 us
  transfers between devices with their start and end apart: 3 -> 17, of which waited for: 3 -> 9; matrix products, arithmetic and copies ran while one was open for 3% -> 31% of each run, Pallas kernels for 0% -> 0%
where the time goes in v1:
time: 504 us; the launch traced here: 500 us
  local copies, waits for them, and re-layouts  175 us (35%)
  blocking collectives  130 us (26%)
  waiting for transfers between devices  129 us (26%)
  starting transfers between devices  23.2 us (5%)
  between operations  17.6 us (3%)
  other arithmetic  14.7 us (3%)
  matrix products  9.11 us (2%)
    dynamic_update_slice x8, local copies, waits for them, and re-layouts, per_device(): lax.dynamic_update_slice_in_dim(column_block, from_left, (position - step...  65.3 us
    unnamed x2, waiting for transfers between devices  63.8 us
    ppermute x8, waiting for transfers between devices, per_device(): from_left = lax.ppermute(from_left, 'tensor', ahead)  60.1 us
    dynamic_update_slice x7, local copies, waits for them, and re-layouts, per_device(): lax.dynamic_update_slice_in_dim(column_block, from_right, (position + ste...  58.3 us
    unnamed x1, blocking collectives  49.8 us
    psum x1, blocking collectives, per_device(): slots = lax.psum(jnp.concatenate([err_part, pow_part], axis=1), 'tensor')  45.7 us
    all_to_all x1, blocking collectives, per_device(): lax.all_to_all(outgoing, 'expert', split_axis=0, concat_axis=0, tiled=True)  34.9 us
    ppermute x7, starting transfers between devices, per_device(): from_right = lax.ppermute(from_right, 'tensor', downward)  17.6 us
  transfers between devices with their start and end apart: 17, of which 9 were waited for; matrix products, arithmetic and copies ran while one was open for 31% of the time, Pallas kernels for 0%

profile of v1, /device:TPU:2, one launch (start us, length us, event | category | flops | bytes accessed | tf_op | source)
XLA Modules:
  0.0 499.5 jit_solution(2733963562140236434)
XLA Ops:
  7.2 2.7 copy.99
  11.0 1.2 reduce-window.6
  14.1 63.8 %reduce-scatter.4.cloned.1.call-done = bf16[448,64]{1,0:T(8,128)(2,1)} async-done(((bf16[7168,64]{1,0:T(8,128)(2,1)}), bf16[448,64]{1,0:T(8,128)(2,1)}) %reduce-scatter.4.cloned.1.call-update) | async-done | bytes 57360
  78.8 1.2 convolution_convert_fusion
  80.6 34.9 %all_to_all.10 = bf16[32,25,448]{2,1,0:T(8,128)(2,1)} all-to-all(bf16[32,25,448]{2,1,0:T(8,128)(2,1)S(1)} %pad_maximum_fusion), channel_id=1, replica_groups=mesh['expert'=32,'tensor'=16] {'expert'}, dimensions={0} | all-to-all | bytes 1433600 | tf_op jit(solution)/shard_map/all_to_all | solution.py:42
  115.5 1.2 slice.37
  117.0 2.9 collective-permute-start.1
  119.9 8.6 %collective-permute-done = bf16[768,448]{0,1:T(8,128)(2,1)S(1)} collective-permute-done((bf16[768,448]{0,1:T(8,128)(2,1)S(1)}, bf16[768,448]{0,1:T(8,128)(2,1)S(1)}, u32[]{:S(2)}, u32[]{:S(2)}) %collective-permute-start) | collective-permute-done | bytes 688160 | tf_op jit(solution)/shard_map/ppermute | solution.py:57
  128.6 3.1 collective-permute-start.3
  131.6 8.5 %collective-permute-done.2 = bf16[768,448]{0,1:T(8,128)(2,1)S(1)} collective-permute-done((bf16[768,448]{0,1:T(8,128)(2,1)S(1)}, bf16[768,448]{0,1:T(8,128)(2,1)S(1)}, u32[]{:S(2)}, u32[]{:S(2)}) %collective-permute-start.2) | collective-permute-done | bytes 688160 | tf_op jit(solution)/shard_map/ppermute | solution.py:57
  141.0 3.0 collective-permute-start.5
  143.9 8.6 %collective-permute-done.4 = bf16[768,448]{0,1:T(8,128)(2,1)S(1)} collective-permute-done((bf16[768,448]{0,1:T(8,128)(2,1)S(1)}, bf16[768,448]{0,1:T(8,128)(2,1)S(1)}, u32[]{:S(2)}, u32[]{:S(2)}) %collective-permute-start.4) | collective-permute-done | bytes 688160 | tf_op jit(solution)/shard_map/ppermute | solution.py:57
  153.4 2.1 collective-permute-start.7
  155.5 8.6 %collective-permute-done.6 = bf16[768,448]{0,1:T(8,128)(2,1)S(1)} collective-permute-done((bf16[768,448]{0,1:T(8,128)(2,1)S(1)}, bf16[768,448]{0,1:T(8,128)(2,1)S(1)}, u32[]{:S(2)}, u32[]{:S(2)}) %collective-permute-start.6) | collective-permute-done | bytes 688160 | tf_op jit(solution)/shard_map/ppermute | solution.py:57
  165.0 2.1 collective-permute-start.9
  167.1 8.6 %collective-permute-done.8 = bf16[768,448]{0,1:T(8,128)(2,1)S(1)} collective-permute-done((bf16[768,448]{0,1:T(8,128)(2,1)S(1)}, bf16[768,448]{0,1:T(8,128)(2,1)S(1)}, u32[]{:S(2)}, u32[]{:S(2)}) %collective-permute-start.8) | collective-permute-done | bytes 688160 | tf_op jit(solution)/shard_map/ppermute | solution.py:57
  176.6 2.1 collective-permute-start.11
  178.7 8.6 %collective-permute-done.10 = bf16[768,448]{0,1:T(8,128)(2,1)S(1)} collective-permute-done((bf16[768,448]{0,1:T(8,128)(2,1)S(1)}, bf16[768,448]{0,1:T(8,128)(2,1)S(1)}, u32[]{:S(2)}, u32[]{:S(2)}) %collective-permute-start.10) | collective-permute-done | bytes 688160 | tf_op jit(solution)/shard_map/ppermute | solution.py:57
  188.1 2.2 collective-permute-start.13
  190.4 8.6 %collective-permute-done.12 = bf16[768,448]{0,1:T(8,128)(2,1)} collective-permute-done((bf16[768,448]{0,1:T(8,128)(2,1)S(1)}, bf16[768,448]{0,1:T(8,128)(2,1)}, u32[]{:S(2)}, u32[]{:S(2)}) %collective-permute-start.12) | collective-permute-done | bytes 688160 | tf_op jit(solution)/shard_map/ppermute | solution.py:57
  199.0 1.3 dynamic-slice
  201.2 49.8 %all-reduce = bf16[7168]{0:T(1024)(128)(2,1)S(1)} all-reduce(bf16[7168]{0:T(1024)(128)(2,1)S(1)} %dynamic-update-slice), channel_id=1, replica_groups=mesh['expert'=32,'tensor'=16] {'tensor'}, use_global_device_ids=true, to_apply=%add | all-reduce | flops 7168 | bytes 28672
  251.1 5.5 %broadcast_in_dim.8 = bf16[768,7168]{1,0:T(8,128)(2,1)} broadcast(bf16[]{:T(256)} %constant.114.clone.1), dimensions={} | broadcast | bytes 11010050 | tf_op jit(solution)/shard_map/broadcast_in_dim | solution.py:48
  256.6 7.9 %dynamic_update_slice.48 = bf16[768,7168]{1,0:T(8,128)(2,1)} dynamic-update-slice(bf16[768,7168]{1,0:T(8,128)(2,1)} %broadcast_in_dim.8, bf16[768,448]{1,0:T(8,128)(2,1)S(1)} %bitcast.40, s32[]{:T(128)} %constant.116.clone.1, s32[]{:T(128)S(6)} %select_n.118) | dynamic-update-slice | bytes 1376260 | tf_op jit(solution)/shard_map/dynamic_update_slice | solution.py:51
  264.5 1.5 fusion.30
  266.0 1.4 copy.75
  267.3 8.0 %dynamic_update_slice.49 = bf16[768,7168]{1,0:T(8,128)(2,1)} dynamic-update-slice(bf16[768,7168]{1,0:T(8,128)(2,1)} %dynamic_update_slice.48, bf16[768,448]{1,0:T(8,128)(2,1)S(1)} %copy.75, s32[]{:T(128)} %constant.116.clone.1, s32[]{:T(128)S(6)} %select_n.120) | dynamic-update-slice | bytes 1376260 | tf_op jit(solution)/shard_map/dynamic_update_slice | solution.py:58
  275.3 1.4 copy.77
  276.7 8.7 %dynamic_update_slice.50 = bf16[768,7168]{1,0:T(8,128)(2,1)} dynamic-update-slice(bf16[768,7168]{1,0:T(8,128)(2,1)} %dynamic_update_slice.49, bf16[768,448]{1,0:T(8,128)(2,1)S(1)} %copy.77, s32[]{:T(128)} %constant.116.clone.1, s32[]{:T(128)S(6)} %select_n.122) | dynamic-update-slice | bytes 1376260 | tf_op jit(solution)/shard_map/dynamic_update_slice | solution.py:63
  285.4 1.4 copy.78
  286.8 7.7 %dynamic_update_slice.51 = bf16[768,7168]{1,0:T(8,128)(2,1)} dynamic-update-slice(bf16[768,7168]{1,0:T(8,128)(2,1)} %dynamic_update_slice.50, bf16[768,448]{1,0:T(8,128)(2,1)S(1)} %copy.78, s32[]{:T(128)} %constant.116.clone.1, s32[]{:T(128)S(6)} %select_n.124) | dynamic-update-slice | bytes 1376260 | tf_op jit(solution)/shard_map/dynamic_update_slice | solution.py:58
  294.5 1.4 copy.79
  295.9 7.9 %dynamic_update_slice.52 = bf16[768,7168]{1,0:T(8,128)(2,1)} dynamic-update-slice(bf16[768,7168]{1,0:T(8,128)(2,1)} %dynamic_update_slice.51, bf16[768,448]{1,0:T(8,128)(2,1)S(1)} %copy.79, s32[]{:T(128)} %constant.116.clone.1, s32[]{:T(128)S(6)} %select_n.126) | dynamic-update-slice | bytes 1376260 | tf_op jit(solution)/shard_map/dynamic_update_slice | solution.py:63
  303.9 1.4 copy.80
  305.2 8.7 %dynamic_update_slice.53 = bf16[768,7168]{1,0:T(8,128)(2,1)} dynamic-update-slice(bf16[768,7168]{1,0:T(8,128)(2,1)} %dynamic_update_slice.52, bf16[768,448]{1,0:T(8,128)(2,1)S(1)} %copy.80, s32[]{:T(128)} %constant.116.clone.1, s32[]{:T(128)S(6)} %select_n.128) | dynamic-update-slice | bytes 1376260 | tf_op jit(solution)/shard_map/dynamic_update_slice | solution.py:58
  313.9 1.4 copy.81
  315.3 8.7 %dynamic_update_slice.54 = bf16[768,7168]{1,0:T(8,128)(2,1)} dynamic-update-slice(bf16[768,7168]{1,0:T(8,128)(2,1)} %dynamic_update_slice.53, bf16[768,448]{1,0:T(8,128)(2,1)S(1)} %copy.81, s32[]{:T(128)} %constant.116.clone.1, s32[]{:T(128)S(6)} %select_n.130) | dynamic-update-slice | bytes 1376260 | tf_op jit(solution)/shard_map/dynamic_update_slice | solution.py:63
  324.0 1.4 copy.82
  325.4 7.8 %dynamic_update_slice.55 = bf16[768,7168]{1,0:T(8,128)(2,1)} dynamic-update-slice(bf16[768,7168]{1,0:T(8,128)(2,1)} %dynamic_update_slice.54, bf16[768,448]{1,0:T(8,128)(2,1)S(1)} %copy.82, s32[]{:T(128)} %constant.116.clone.1, s32[]{:T(128)S(6)} %select_n.132) | dynamic-update-slice | bytes 1376260 | tf_op jit(solution)/shard_map/dynamic_update_slice | solution.py:58
  333.5 7.8 %dynamic_update_slice.56 = bf16[768,7168]{1,0:T(8,128)(2,1)} dynamic-update-slice(bf16[768,7168]{1,0:T(8,128)(2,1)} %dynamic_update_slice.55, bf16[768,448]{1,0:T(8,128)(2,1)S(1)} %copy.83, s32[]{:T(128)} %constant.116.clone.1, s32[]{:T(128)S(6)} %select_n.134) | dynamic-update-slice | bytes 1376260 | tf_op jit(solution)/shard_map/dynamic_update_slice | solution.py:63
  341.3 1.4 copy.84
  342.7 8.7 %dynamic_update_slice.57 = bf16[768,7168]{1,0:T(8,128)(2,1)} dynamic-update-slice(bf16[768,7168]{1,0:T(8,128)(2,1)} %dynamic_update_slice.56, bf16[768,448]{1,0:T(8,128)(2,1)S(1)} %copy.84, s32[]{:T(128)} %constant.116.clone.1, s32[]{:T(128)S(6)} %select_n.136) | dynamic-update-slice | bytes 1376260 | tf_op jit(solution)/shard_map/dynamic_update_slice | solution.py:58
  351.4 1.4 copy.85
  352.7 8.7 %dynamic_update_slice.58 = bf16[768,7168]{1,0:T(8,128)(2,1)} dynamic-update-slice(bf16[768,7168]{1,0:T(8,128)(2,1)} %dynamic_update_slice.57, bf16[768,448]{1,0:T(8,128)(2,1)S(1)} %copy.85, s32[]{:T(128)} %constant.116.clone.1, s32[]{:T(128)S(6)} %select_n.138) | dynamic-update-slice | bytes 1376260 | tf_op jit(solution)/shard_map/dynamic_update_slice | solution.py:63
  361.4 1.4 copy.86
  362.8 7.9 %dynamic_update_slice.59 = bf16[768,7168]{1,0:T(8,128)(2,1)} dynamic-update-slice(bf16[768,7168]{1,0:T(8,128)(2,1)} %dynamic_update_slice.58, bf16[768,448]{1,0:T(8,128)(2,1)S(1)} %copy.86, s32[]{:T(128)} %constant.116.clone.1, s32[]{:T(128)S(6)} %select_n.140) | dynamic-update-slice | bytes 1376260 | tf_op jit(solution)/shard_map/dynamic_update_slice | solution.py:58
  370.6 1.4 copy.87
  372.0 7.9 %dynamic_update_slice.60 = bf16[768,7168]{1,0:T(8,128)(2,1)} dynamic-update-slice(bf16[768,7168]{1,0:T(8,128)(2,1)} %dynamic_update_slice.59, bf16[768,448]{1,0:T(8,128)(2,1)S(1)} %copy.87, s32[]{:T(128)} %constant.116.clone.1, s32[]{:T(128)S(6)} %select_n.142) | dynamic-update-slice | bytes 1376260 | tf_op jit(solution)/shard_map/dynamic_update_slice | solution.py:63
  379.9 1.4 copy.88
  381.3 8.7 %dynamic_update_slice.61 = bf16[768,7168]{1,0:T(8,128)(2,1)} dynamic-update-slice(bf16[768,7168]{1,0:T(8,128)(2,1)} %dynamic_update_slice.60, bf16[768,448]{1,0:T(8,128)(2,1)S(1)} %copy.88, s32[]{:T(128)} %constant.116.clone.1, s32[]{:T(128)S(6)} %select_n.144) | dynamic-update-slice | bytes 1376260 | tf_op jit(solution)/shard_map/dynamic_update_slice | solution.py:58
  390.0 1.4 copy.89
  391.3 8.7 %dynamic_update_slice.62 = bf16[768,7168]{1,0:T(8,128)(2,1)} dynamic-update-slice(bf16[768,7168]{1,0:T(8,128)(2,1)} %dynamic_update_slice.61, bf16[768,448]{1,0:T(8,128)(2,1)S(1)} %copy.89, s32[]{:T(128)} %constant.116.clone.1, s32[]{:T(128)S(6)} %select_n.146) | dynamic-update-slice | bytes 1376260 | tf_op jit(solution)/shard_map/dynamic_update_slice | solution.py:63
  400.0 1.4 copy.90
  401.4 7.9 %dynamic_update_slice.63 = bf16[768,7168]{1,0:T(8,128)(2,1)} dynamic-update-slice(bf16[768,7168]{1,0:T(8,128)(2,1)} %dynamic_update_slice.62, bf16[768,448]{1,0:T(8,128)(2,1)S(1)} %copy.90, s32[]{:T(128)} %constant.116.clone.1, s32[]{:T(128)S(6)} %select_n.148) | dynamic-update-slice | bytes 1376260 | tf_op jit(solution)/shard_map/dynamic_update_slice | solution.py:58
  409.3 6.5 %fusion = f32[768]{0:T(1024)S(1)} fusion(bf16[768,7168]{1,0:T(8,128)(2,1)} %dynamic_update_slice.63), kind=kLoop, calls=%fused_computation.4 | loop fusion | flops 16514304 | bytes 11013120 | tf_op jit(solution)/shard_map/reduce_sum | solution.py:67
  415.8 1.5 fusion.9
  417.3 3.9 multiply_reduce_fusion
  421.2 4.0 fusion.20
  425.4 45.7 %psum.7 = f32[32,2,24]{2,0,1:T(8,128)S(1)} all-reduce(f32[32,2,24]{2,0,1:T(8,128)S(1)} %pad_maximum_fusion.1), channel_id=1, replica_groups=mesh['expert'=32,'tensor'=16] {'tensor'}, use_global_device_ids=true, to_apply=%region_9.10 | all-reduce | flops 1536 | bytes 12288 | tf_op jit(solution)/shard_map/psum | solution.py:80
  471.7 5.6 %all-to-all-start.1 = ((f32[32,2,24]{2,1,0:T(2,128)}), f32[32,2,24]{2,1,0:T(2,128)S(1)}, u32[]{:S(2)}, u32[]{:S(2)}) async-start(f32[32,2,24]{2,1,0:T(2,128)} %copy.91), calls=%async_computation.1 | async-start | bytes 65536 | tf_op jit(solution)/shard_map/all_to_all | solution.py:82
  477.3 1.2 multiply_divide_fusion
  480.4 5.5 %all-to-all-done.1 = f32[32,2,24]{2,1,0:T(2,128)S(1)} async-done(((f32[32,2,24]{2,1,0:T(2,128)}), f32[32,2,24]{2,1,0:T(2,128)S(1)}, u32[]{:S(2)}, u32[]{:S(2)}) %all-to-all-start.1) | async-done | bytes 6176 | tf_op jit(solution)/shard_map/all_to_all | solution.py:82
  486.2 2.3 gather_fusion
  488.5 2.3 gather_fusion.1
  (93 shorter events, 12.0 us)
Async XLA Ops:
  7.2 410.1 %copy-start = (bf16[1,7168,128]{2,1,0:T(8,128)(2,1)S(1)}, bf16[1,7168,128]{2,1,0:T(8,128)(2,1)}, u32[]{:S(2)}) copy-start(bf16[1,7168,128]{2,1,0:T(8,128)(2,1)} %param.14) | copy-start | bytes 5505028
  7.2 191.8 %copy-start.15 = (bf16[448]{0:T(512)(128)(2,1)S(1)}, bf16[448]{0:T(512)(128)(2,1)}, u32[]{:S(2)}) copy-start(bf16[448]{0:T(512)(128)(2,1)} %param.11) | copy-start | bytes 2692
  7.2 243.8 %copy-start.14 = (f32[64,8]{0,1:T(8,128)S(1)}, f32[64,8]{0,1:T(8,128)}, u32[]{:S(2)}) copy-start(f32[64,8]{0,1:T(8,128)} %param.13) | copy-start | bytes 6148
  7.2 70.6 %reduce-scatter.4.cloned.1.call-start = ((), (), s32[]{:S(2)}) async-start(), calls=%async_computation.3 | async-start | bytes 1949696
  116.7 170.1 %copy-start.2 = (bf16[32,24,448]{2,1,0:T(8,128)(2,1)}, bf16[32,24,448]{2,1,0:T(8,128)(2,1)S(1)}, u32[]{:S(2)}) copy-start(bf16[32,24,448]{2,1,0:T(8,128)(2,1)S(1)} %slice.37) | copy-start | bytes 2064388
  117.0 11.6 %collective-permute-start = (bf16[768,448]{0,1:T(8,128)(2,1)S(1)}, bf16[768,448]{0,1:T(8,128)(2,1)S(1)}, u32[]{:S(2)}, u32[]{:S(2)}) collective-permute-start(bf16[768,448]{0,1:T(8,128)(2,1)S(1)} %copy.74), channel_id=1, source_target_pairs={{0,1},{1,2},{2,3},{3,4},{4,5},{5,6},{6,7},{7,8},{8,9},{9,10},{10,1... | collective-permute-start | bytes 2064392 | tf_op jit(solution)/shard_map/ppermute | solution.py:57
  117.0 11.6 %collective-permute-start.1 = (bf16[768,448]{0,1:T(8,128)(2,1)S(1)}, bf16[768,448]{0,1:T(8,128)(2,1)}, u32[]{:S(2)}, u32[]{:S(2)}) collective-permute-start(bf16[768,448]{0,1:T(8,128)(2,1)S(1)} %copy.74), channel_id=1, source_target_pairs={{0,15},{1,0},{2,1},{3,2},{4,3},{5,4},{6,5},{7,6},{8,7},{9,8},{10,9... | collective-permute-start | bytes 2064392 | tf_op jit(solution)/shard_map/ppermute | solution.py:62
  128.5 24.0 %copy-start.4 = (bf16[768,448]{0,1:T(8,128)(2,1)}, bf16[768,448]{0,1:T(8,128)(2,1)S(1)}, u32[]{:S(2)}) copy-start(bf16[768,448]{0,1:T(8,128)(2,1)S(1)} %collective-permute-done) | copy-start | bytes 2064388
  128.5 11.6 %collective-permute-start.2 = (bf16[768,448]{0,1:T(8,128)(2,1)S(1)}, bf16[768,448]{0,1:T(8,128)(2,1)S(1)}, u32[]{:S(2)}, u32[]{:S(2)}) collective-permute-start(bf16[768,448]{0,1:T(8,128)(2,1)S(1)} %collective-permute-done), channel_id=1, source_target_pairs={{0,1},{1,2},{2,3},{3,4},{4,5},{5,6},{6,7},{7,8},{8,9},{9,10},{10,1... | collective-permute-start | bytes 2064392 | tf_op jit(solution)/shard_map/ppermute | solution.py:57
  128.6 12.4 %collective-permute-start.3 = (bf16[768,448]{0,1:T(8,128)(2,1)}, bf16[768,448]{0,1:T(8,128)(2,1)S(1)}, u32[]{:S(2)}, u32[]{:S(2)}) collective-permute-start(bf16[768,448]{0,1:T(8,128)(2,1)} %collective-permute-done.1), channel_id=1, source_target_pairs={{0,15},{1,0},{2,1},{3,2},{4,3},{5,4},{6,5},{7,6},{8,7},{9,8},{10,9... | collective-permute-start | bytes 2064392 | tf_op jit(solution)/shard_map/ppermute | solution.py:62
  140.1 0.8 copy-start.3
  141.0 11.6 %collective-permute-start.4 = (bf16[768,448]{0,1:T(8,128)(2,1)S(1)}, bf16[768,448]{0,1:T(8,128)(2,1)S(1)}, u32[]{:S(2)}, u32[]{:S(2)}) collective-permute-start(bf16[768,448]{0,1:T(8,128)(2,1)S(1)} %collective-permute-done.2), channel_id=1, source_target_pairs={{0,1},{1,2},{2,3},{3,4},{4,5},{5,6},{6,7},{7,8},{8,9},{9,10},{10,1... | collective-permute-start | bytes 2064392 | tf_op jit(solution)/shard_map/ppermute | solution.py:57
  141.0 11.6 %copy-start.5 = (bf16[768,448]{0,1:T(8,128)(2,1)}, bf16[768,448]{0,1:T(8,128)(2,1)S(1)}, u32[]{:S(2)}) copy-start(bf16[768,448]{0,1:T(8,128)(2,1)S(1)} %collective-permute-done.3) | copy-start | bytes 2064388
  141.0 11.6 %collective-permute-start.5 = (bf16[768,448]{0,1:T(8,128)(2,1)S(1)}, bf16[768,448]{0,1:T(8,128)(2,1)S(1)}, u32[]{:S(2)}, u32[]{:S(2)}) collective-permute-start(bf16[768,448]{0,1:T(8,128)(2,1)S(1)} %collective-permute-done.3), channel_id=1, source_target_pairs={{0,15},{1,0},{2,1},{3,2},{4,3},{5,4},{6,5},{7,6},{8,7},{9,8},{10,9... | collective-permute-start | bytes 2064392 | tf_op jit(solution)/shard_map/ppermute | solution.py:62
  152.5 0.8 copy-start.6
  152.5 11.6 %collective-permute-start.6 = (bf16[768,448]{0,1:T(8,128)(2,1)S(1)}, bf16[768,448]{0,1:T(8,128)(2,1)S(1)}, u32[]{:S(2)}, u32[]{:S(2)}) collective-permute-start(bf16[768,448]{0,1:T(8,128)(2,1)S(1)} %collective-permute-done.4), channel_id=1, source_target_pairs={{0,1},{1,2},{2,3},{3,4},{4,5},{5,6},{6,7},{7,8},{8,9},{9,10},{10,1... | collective-permute-start | bytes 2064392 | tf_op jit(solution)/shard_map/ppermute | solution.py:57
  153.4 10.7 %copy-start.7 = (bf16[768,448]{0,1:T(8,128)(2,1)}, bf16[768,448]{0,1:T(8,128)(2,1)S(1)}, u32[]{:S(2)}) copy-start(bf16[768,448]{0,1:T(8,128)(2,1)S(1)} %collective-permute-done.5) | copy-start | bytes 2064388
  153.4 10.7 %collective-permute-start.7 = (bf16[768,448]{0,1:T(8,128)(2,1)S(1)}, bf16[768,448]{0,1:T(8,128)(2,1)S(1)}, u32[]{:S(2)}, u32[]{:S(2)}) collective-permute-start(bf16[768,448]{0,1:T(8,128)(2,1)S(1)} %collective-permute-done.5), channel_id=1, source_target_pairs={{0,15},{1,0},{2,1},{3,2},{4,3},{5,4},{6,5},{7,6},{8,7},{9,8},{10,9... | collective-permute-start | bytes 2064392 | tf_op jit(solution)/shard_map/ppermute | solution.py:62
  164.1 0.9 copy-start.8
  164.1 11.6 %collective-permute-start.8 = (bf16[768,448]{0,1:T(8,128)(2,1)S(1)}, bf16[768,448]{0,1:T(8,128)(2,1)S(1)}, u32[]{:S(2)}, u32[]{:S(2)}) collective-permute-start(bf16[768,448]{0,1:T(8,128)(2,1)S(1)} %collective-permute-done.6), channel_id=1, source_target_pairs={{0,1},{1,2},{2,3},{3,4},{4,5},{5,6},{6,7},{7,8},{8,9},{9,10},{10,1... | collective-permute-start | bytes 2064392 | tf_op jit(solution)/shard_map/ppermute | solution.py:57
  165.0 10.7 %copy-start.9 = (bf16[768,448]{0,1:T(8,128)(2,1)}, bf16[768,448]{0,1:T(8,128)(2,1)S(1)}, u32[]{:S(2)}) copy-start(bf16[768,448]{0,1:T(8,128)(2,1)S(1)} %collective-permute-done.7) | copy-start | bytes 2064388
  165.0 10.7 %collective-permute-start.9 = (bf16[768,448]{0,1:T(8,128)(2,1)S(1)}, bf16[768,448]{0,1:T(8,128)(2,1)S(1)}, u32[]{:S(2)}, u32[]{:S(2)}) collective-permute-start(bf16[768,448]{0,1:T(8,128)(2,1)S(1)} %collective-permute-done.7), channel_id=1, source_target_pairs={{0,15},{1,0},{2,1},{3,2},{4,3},{5,4},{6,5},{7,6},{8,7},{9,8},{10,9... | collective-permute-start | bytes 2064392 | tf_op jit(solution)/shard_map/ppermute | solution.py:62
  175.7 0.9 copy-start.11
  175.7 11.6 %collective-permute-start.10 = (bf16[768,448]{0,1:T(8,128)(2,1)S(1)}, bf16[768,448]{0,1:T(8,128)(2,1)S(1)}, u32[]{:S(2)}, u32[]{:S(2)}) collective-permute-start(bf16[768,448]{0,1:T(8,128)(2,1)S(1)} %collective-permute-done.8), channel_id=1, source_target_pairs={{0,1},{1,2},{2,3},{3,4},{4,5},{5,6},{6,7},{7,8},{8,9},{9,10},{10,1... | collective-permute-start | bytes 2064392 | tf_op jit(solution)/shard_map/ppermute | solution.py:57
  176.6 10.7 %copy-start.12 = (bf16[768,448]{0,1:T(8,128)(2,1)}, bf16[768,448]{0,1:T(8,128)(2,1)S(1)}, u32[]{:S(2)}) copy-start(bf16[768,448]{0,1:T(8,128)(2,1)S(1)} %collective-permute-done.9) | copy-start | bytes 2064388
  176.6 10.7 %collective-permute-start.11 = (bf16[768,448]{0,1:T(8,128)(2,1)S(1)}, bf16[768,448]{0,1:T(8,128)(2,1)}, u32[]{:S(2)}, u32[]{:S(2)}) collective-permute-start(bf16[768,448]{0,1:T(8,128)(2,1)S(1)} %collective-permute-done.9), channel_id=1, source_target_pairs={{0,15},{1,0},{2,1},{3,2},{4,3},{5,4},{6,5},{7,6},{8,7},{9,8},{10,9... | collective-permute-start | bytes 2064392 | tf_op jit(solution)/shard_map/ppermute | solution.py:62
  187.3 0.9 copy-start.13
  187.3 11.7 %collective-permute-start.12 = (bf16[768,448]{0,1:T(8,128)(2,1)S(1)}, bf16[768,448]{0,1:T(8,128)(2,1)}, u32[]{:S(2)}, u32[]{:S(2)}) collective-permute-start(bf16[768,448]{0,1:T(8,128)(2,1)S(1)} %collective-permute-done.10), channel_id=1, source_target_pairs={{0,1},{1,2},{2,3},{3,4},{4,5},{5,6},{6,7},{7,8},{8,9},{9,10},{10,1... | collective-permute-start | bytes 2064392 | tf_op jit(solution)/shard_map/ppermute | solution.py:57
  188.1 201.8 %collective-permute-start.13 = (bf16[768,448]{0,1:T(8,128)(2,1)}, bf16[768,448]{0,1:T(8,128)(2,1)}, u32[]{:S(2)}, u32[]{:S(2)}) collective-permute-start(bf16[768,448]{0,1:T(8,128)(2,1)} %collective-permute-done.11), channel_id=1, source_target_pairs={{0,15},{1,0},{2,1},{3,2},{4,3},{5,4},{6,5},{7,6},{8,7},{9,8},{10,9... | collective-permute-start | bytes 2064392 | tf_op jit(solution)/shard_map/ppermute | solution.py:62
  199.0 201.1 %collective-permute-start.14 = (bf16[768,448]{0,1:T(8,128)(2,1)}, bf16[768,448]{0,1:T(8,128)(2,1)}, u32[]{:S(2)}, u32[]{:S(2)}) collective-permute-start(bf16[768,448]{0,1:T(8,128)(2,1)} %collective-permute-done.12), channel_id=1, source_target_pairs={{0,1},{1,2},{2,3},{3,4},{4,5},{5,6},{6,7},{7,8},{8,9},{9,10},{10,1... | collective-permute-start | bytes 2064392 | tf_op jit(solution)/shard_map/ppermute | solution.py:57
  294.5 38.7 %copy-start.10 = (bf16[768,448]{0,1:T(8,128)(2,1)S(1)}, bf16[768,448]{0,1:T(8,128)(2,1)}, u32[]{:S(2)}) copy-start(bf16[768,448]{0,1:T(8,128)(2,1)} %copy-done.9) | copy-start | bytes 2064388
  409.3 8.0 %copy-start.1 = (bf16[768,7168]{1,0:T(8,128)(2,1)S(1)}, bf16[768,7168]{1,0:T(8,128)(2,1)}, u32[]{:S(2)}) copy-start(bf16[768,7168]{1,0:T(8,128)(2,1)} %dynamic_update_slice.63) | copy-start | bytes 33030148
  417.3 3.9 copy-start.16
  471.7 14.2 %all-to-all-start.1 = ((f32[32,2,24]{2,1,0:T(2,128)}), f32[32,2,24]{2,1,0:T(2,128)S(1)}, u32[]{:S(2)}, u32[]{:S(2)}) async-start(f32[32,2,24]{2,1,0:T(2,128)} %copy.91), calls=%async_computation.1 | async-start | bytes 65536 | tf_op jit(solution)/shard_map/all_to_all | solution.py:82
Sparse Core Ops, SparseCore 0:
  10.9 66.9 reduce-scatter.3
